TPU v7x, 512 devices: a whole 4x8x8 slice. The times are simulated.
512 devices in a mesh: row: 32 (over x, y), col: 16 (over z, core).
Axes of the slice: x: 4, y: 8, z: 8, core: 2. Of those that a mesh axis runs over, the one named last changes fastest.
Arguments:
- factor_rows: bfloat16 [2, 1024, 262144], P(None, None, ('row', 'col')), may hold values from -0.046875 to 0.046875
- solved: bfloat16 [64, 262144], P(None, ('row', 'col')), may hold values from -6 to 6
- inverses: bfloat16 [2, 1024, 1024], P(None, 'row', 'col'), as said below
- link_tile: bfloat16 [1024, 1024], P('col', 'row'), may hold values from -0.1875 to 0.1875
- right_side: float32 [2, 1024, 64], P(None, 'col'), may hold values from -6 to 6
Outputs:
- back_solved: float32 [2, 1024, 64], P(None, 'col')
- remaining: float32 [64, 262144], P(None, ('row', 'col'))
Inputs may be any that keep to these rules, and one draw needn't show every extreme that they name: `inverses`: each of the two blocks is lower triangular with a positive diagonal.
All inputs are finite; a program needn't handle non-finite values.
Results may differ from a plain program's by a relative error of at most 0.015.
Values may be sent and summed in bfloat16 or wider, within the bound.
A program may use at most 64 MiB of HBM per device.

v0:
```python
import jax
import jax.numpy as jnp
from jax import lax
from jax.sharding import PartitionSpec as P


def in_blocks(shard, dim, devices):
    shape = shard.shape
    tiles = shard.reshape(*shape[:dim], devices, shape[dim] // devices, *shape[dim + 1 :])
    return jnp.moveaxis(tiles, dim, 0)


def sum_at_owner(shard, axis, dim):
    tiles = in_blocks(shard, dim, lax.axis_size(axis))
    arrived = lax.all_to_all(tiles, axis, split_axis=0, concat_axis=0, tiled=True)
    return arrived.sum(axis=0)


def sent_to_all(shard, axis):
    devices = lax.axis_size(axis)
    return lax.all_to_all(
        jnp.broadcast_to(shard[None], (devices, *shard.shape)), axis, 0, 0, tiled=True
    )


def over_copies(shard, axis):
    return sent_to_all(shard, axis).astype(jnp.float32).sum(axis=0)


def of_everyone(shard, axis):
    return sent_to_all(shard, axis).sum(axis=0)


def in_order(tiles, dim):
    shape = list(tiles.shape[1:])
    shape[dim] *= tiles.shape[0]
    return jnp.moveaxis(tiles, 0, dim).reshape(shape)


def gathered_copies(shard, axis, dim):
    tiles = sent_to_all(shard, axis)
    return in_order(tiles, dim)


def shards(factor_rows, solved, inverses, link_tile, right_side):
    partial_value = jnp.einsum(
        "kic,nc->kin", factor_rows, solved, preferred_element_type=jnp.float32
    )
    column_part = sum_at_owner(partial_value, "col", 1)
    panel_sum = over_copies(column_part.astype(jnp.bfloat16), "row").astype(jnp.float32)

    def forward_solve(which, residue):
        rows_part = jnp.dot(inverses[which], residue, preferred_element_type=jnp.float32)
        solved_rows = of_everyone(rows_part, "col").astype(jnp.bfloat16)
        return (solved_rows, solved_rows)

    residue_first = (right_side[0] - panel_sum[0]).astype(jnp.bfloat16)
    first_all, first_rows = forward_solve(0, residue_first)
    link_part = jnp.dot(link_tile, first_rows, preferred_element_type=jnp.float32)
    link_sum = of_everyone(link_part, "row")
    residue_last = (right_side[1] - panel_sum[1] - link_sum).astype(jnp.bfloat16)
    last_all, last_rows = forward_solve(1, residue_last)

    def transpose_solve(which, vector_rows):
        product = jnp.einsum(
            "ij,in->jn", inverses[which], vector_rows, preferred_element_type=jnp.float32
        )
        return of_everyone(product, "row")

    last_out = transpose_solve(1, last_rows)
    last_short = last_out.astype(jnp.bfloat16)
    last_short_all = gathered_copies(last_short, "col", 0)
    update_last = jnp.einsum(
        "iw,in->nw", factor_rows[1], last_short_all, preferred_element_type=jnp.float32
    )
    back_part = jnp.einsum("ji,jn->in", link_tile, last_short, preferred_element_type=jnp.float32)
    back_sum = of_everyone(back_part, "col")
    carry_rows = (first_rows.astype(jnp.float32) - back_sum).astype(jnp.bfloat16)
    first_out = transpose_solve(0, carry_rows)
    first_short = first_out.astype(jnp.bfloat16)
    first_short_all = gathered_copies(first_short, "col", 0)
    update = update_last + jnp.einsum(
        "iw,in->nw", factor_rows[0], first_short_all, preferred_element_type=jnp.float32
    )
    remaining = solved.astype(jnp.float32) - update
    back_solved = jnp.stack([first_out, last_out])
    return (back_solved, remaining)


def solution(mesh):
    placed = (
        P(None, None, ("row", "col")),
        P(None, ("row", "col")),
        P(None, "row", "col"),
        P("col", "row"),
        P(None, "col", None),
    )
    return jax.shard_map(
        shards,
        mesh=mesh,
        in_specs=placed,
        out_specs=(P(None, "col", None), P(None, ("row", "col"))),
        check_vma=False,
    )
```

profile of v0, /device:TPU:1, one launch (start us, length us, event | category | flops | bytes accessed | tf_op | source)
XLA Modules:
  0.0 211.6 jit_solution(17111025326186318607)
XLA Ops:
  0.6 2.3 %fusion.6 = f32[2,1024,64]{1,2,0:T(8,128)S(1)} fusion(bf16[2,1024,512]{2,1,0:T(8,128)(2,1)} %param.5, bf16[64,512]{1,0:T(8,128)(2,1)} %param.6), kind=kOutput, calls=%fused_computation.16 | convolution fusion | flops 134217728 | bytes 2686976 | tf_op jit(solution)/shard_map/kic,nc->kin/dot_general | solution.py:46
  4.3 28.8 %all_to_all.50 = f32[16,1,8192]{2,1,0:T(1,128)S(1)} all-to-all(f32[16,1,8192]{2,1,0:T(1,128)S(1)} %reshape.35), channel_id=1, replica_groups=mesh['row'=32,'col'=16] {'col'}, dimensions={0} | all-to-all | bytes 1048576 | tf_op jit(solution)/shard_map/all_to_all | solution.py:15
  33.6 1.9 reduce
  36.4 0.8 reshape.37
  37.2 26.2 %all_to_all.51 = bf16[32,2,4096]{2,1,0:T(2,128)(2,1)S(1)} all-to-all(bf16[32,2,4096]{2,1,0:T(2,128)(2,1)S(1)} %reshape.37), channel_id=1, replica_groups=mesh['row'=32,'col'=16] {'row'}, dimensions={0} | all-to-all | bytes 1048576 | tf_op jit(solution)/shard_map/all_to_all | solution.py:21
  63.4 0.7 reshape.38
  64.7 12.3 %all_to_all.52 = f32[16,1,2048]{2,1,0:T(1,128)S(1)} all-to-all(f32[16,1,2048]{2,1,0:T(1,128)S(1)} %reshape.39), channel_id=1, replica_groups=mesh['row'=32,'col'=16] {'col'}, dimensions={0} | all-to-all | bytes 262144 | tf_op jit(solution)/shard_map/all_to_all | solution.py:21
  77.0 1.0 reduce.1
  78.5 0.7 reshape.41
  79.2 20.2 %all_to_all.53 = f32[32,1,4096]{2,1,0:T(1,128)S(1)} all-to-all(f32[32,1,4096]{2,1,0:T(1,128)S(1)} %reshape.41), channel_id=1, replica_groups=mesh['row'=32,'col'=16] {'row'}, dimensions={0} | all-to-all | bytes 1048576 | tf_op jit(solution)/shard_map/all_to_all | solution.py:21
  99.4 1.9 reduce.2
  102.2 14.4 %all_to_all.54 = f32[16,1,2048]{2,1,0:T(1,128)S(1)} all-to-all(f32[16,1,2048]{2,1,0:T(1,128)S(1)} %reshape.43), channel_id=1, replica_groups=mesh['row'=32,'col'=16] {'col'}, dimensions={0} | all-to-all | bytes 262144 | tf_op jit(solution)/shard_map/all_to_all | solution.py:21
  116.6 1.0 reduce.3
  118.1 0.7 reshape.45
  118.7 21.6 %all_to_all.55 = f32[32,1,4096]{2,1,0:T(1,128)S(1)} all-to-all(f32[32,1,4096]{2,1,0:T(1,128)S(1)} %reshape.45), channel_id=1, replica_groups=mesh['row'=32,'col'=16] {'row'}, dimensions={0} | all-to-all | bytes 1048576 | tf_op jit(solution)/shard_map/all_to_all | solution.py:21
  140.3 1.9 reduce.4
  143.0 0.8 reshape.47
  143.8 4.6 %all-to-all-start.6 = ((f32[16,1,2048]{2,1,0:T(1,128)}), f32[16,1,2048]{2,1,0:T(1,128)S(1)}, u32[]{:S(2)}, u32[]{:S(2)}) async-start(f32[16,1,2048]{2,1,0:T(1,128)} %reshape.47), calls=%async_computation.6 | async-start | bytes 262144 | tf_op jit(solution)/shard_map/all_to_all | solution.py:21
  148.4 0.9 reshape.51
  149.3 8.2 %all-to-all-done.6 = f32[16,1,2048]{2,1,0:T(1,128)S(1)} async-done(((f32[16,1,2048]{2,1,0:T(1,128)}), f32[16,1,2048]{2,1,0:T(1,128)S(1)}, u32[]{:S(2)}, u32[]{:S(2)}) %all-to-all-start.6) | async-done | bytes 131104 | tf_op jit(solution)/shard_map/all_to_all | solution.py:21
  157.6 3.4 %all-to-all-start.8 = ((bf16[16,2,2048]{2,1,0:T(2,128)(2,1)}), bf16[16,2,2048]{2,1,0:T(2,128)(2,1)S(1)}, u32[]{:S(2)}, u32[]{:S(2)}) async-start(bf16[16,2,2048]{2,1,0:T(2,128)(2,1)} %reshape.51), calls=%async_computation.8 | async-start | bytes 262144 | tf_op jit(solution)/shard_map/all_to_all | solution.py:21
  161.0 1.0 reduce.5
  162.5 1.4 reshape.49
  163.9 5.5 %all-to-all-done.8 = bf16[16,2,2048]{2,1,0:T(2,128)(2,1)S(1)} async-done(((bf16[16,2,2048]{2,1,0:T(2,128)(2,1)}), bf16[16,2,2048]{2,1,0:T(2,128)(2,1)S(1)}, u32[]{:S(2)}, u32[]{:S(2)}) %all-to-all-start.8) | async-done | bytes 131104 | tf_op jit(solution)/shard_map/all_to_all | solution.py:21
  169.4 5.4 %all-to-all-start.7 = ((f32[32,1,4096]{2,1,0:T(1,128)}), f32[32,1,4096]{2,1,0:T(1,128)S(1)}, u32[]{:S(2)}, u32[]{:S(2)}) async-start(f32[32,1,4096]{2,1,0:T(1,128)} %reshape.49), calls=%async_computation.7 | async-start | bytes 1048576 | tf_op jit(solution)/shard_map/all_to_all | solution.py:21
  175.1 14.6 %all-to-all-done.7 = f32[32,1,4096]{2,1,0:T(1,128)S(1)} async-done(((f32[32,1,4096]{2,1,0:T(1,128)}), f32[32,1,4096]{2,1,0:T(1,128)S(1)}, u32[]{:S(2)}, u32[]{:S(2)}) %all-to-all-start.7) | async-done | bytes 524320 | tf_op jit(solution)/shard_map/all_to_all | solution.py:21
  189.7 2.8 %reduce.6 = f32[32,4096]{1,0:T(8,128)} reduce(f32[32,1,4096]{2,1,0:T(1,128)S(1)} %all-to-all-done.7, f32[]{:T(128)} %broadcast.16), dimensions={1}, to_apply=%all_to_all.37.reduce_sub_computation | reduce | bytes 1048580 | tf_op jit(solution)/shard_map/all_to_all | solution.py:21
  192.5 1.5 reshape.50
  194.2 0.9 reshape.53
  195.1 6.2 %all-to-all-start.9 = ((bf16[16,2,2048]{2,1,0:T(2,128)(2,1)}), bf16[16,2,2048]{2,1,0:T(2,128)(2,1)S(1)}, u32[]{:S(2)}, u32[]{:S(2)}) async-start(bf16[16,2,2048]{2,1,0:T(2,128)(2,1)} %reshape.53), calls=%async_computation.9 | async-start | bytes 262144 | tf_op jit(solution)/shard_map/all_to_all | solution.py:21
  202.2 8.2 %all-to-all-done.9 = bf16[16,2,2048]{2,1,0:T(2,128)(2,1)S(1)} async-done(((bf16[16,2,2048]{2,1,0:T(2,128)(2,1)}), bf16[16,2,2048]{2,1,0:T(2,128)(2,1)S(1)}, u32[]{:S(2)}, u32[]{:S(2)}) %all-to-all-start.9) | async-done | bytes 131104 | tf_op jit(solution)/shard_map/all_to_all | solution.py:21
  210.7 1.0 fusion
  (55 shorter events, 7.8 us)
Async XLA Ops:
  0.6 77.5 %copy-start = (bf16[64,32]{0,1:T(8,128)(2,1)S(1)}, bf16[64,32]{0,1:T(8,128)(2,1)}, u32[]{:S(2)}) copy-start(bf16[64,32]{0,1:T(8,128)(2,1)} %param.8) | copy-start | bytes 12292
  37.2 27.1 %copy-start.3 = (f32[2,64,64]{2,1,0:T(8,128)S(1)}, f32[2,64,64]{2,1,0:T(8,128)}, u32[]{:S(2)}) copy-start(f32[2,64,64]{2,1,0:T(8,128)} %param.9) | copy-start | bytes 98308
  37.2 27.1 %copy-start.4 = (bf16[2,32,64]{2,1,0:T(8,128)(2,1)S(1)}, bf16[2,32,64]{2,1,0:T(8,128)(2,1)}, u32[]{:S(2)}) copy-start(bf16[2,32,64]{2,1,0:T(8,128)(2,1)} %param.7) | copy-start | bytes 24580
  143.8 13.8 %all-to-all-start.6 = ((f32[16,1,2048]{2,1,0:T(1,128)}), f32[16,1,2048]{2,1,0:T(1,128)S(1)}, u32[]{:S(2)}, u32[]{:S(2)}) async-start(f32[16,1,2048]{2,1,0:T(1,128)} %reshape.47), calls=%async_computation.6 | async-start | bytes 262144 | tf_op jit(solution)/shard_map/all_to_all | solution.py:21
  157.6 11.9 %all-to-all-start.8 = ((bf16[16,2,2048]{2,1,0:T(2,128)(2,1)}), bf16[16,2,2048]{2,1,0:T(2,128)(2,1)S(1)}, u32[]{:S(2)}, u32[]{:S(2)}) async-start(bf16[16,2,2048]{2,1,0:T(2,128)(2,1)} %reshape.51), calls=%async_computation.8 | async-start | bytes 262144 | tf_op jit(solution)/shard_map/all_to_all | solution.py:21
  169.4 20.3 %all-to-all-start.7 = ((f32[32,1,4096]{2,1,0:T(1,128)}), f32[32,1,4096]{2,1,0:T(1,128)S(1)}, u32[]{:S(2)}, u32[]{:S(2)}) async-start(f32[32,1,4096]{2,1,0:T(1,128)} %reshape.49), calls=%async_computation.7 | async-start | bytes 1048576 | tf_op jit(solution)/shard_map/all_to_all | solution.py:21
  175.1 26.2 %copy-start.1 = (bf16[2,1024,512]{2,1,0:T(8,128)(2,1)S(1)}, bf16[2,1024,512]{2,1,0:T(8,128)(2,1)}, u32[]{:S(2)}) copy-start(bf16[2,1024,512]{2,1,0:T(8,128)(2,1)} %param.5) | copy-start | bytes 6291460
  194.0 16.7 %copy-start.2 = (bf16[64,512]{1,0:T(8,128)(2,1)S(1)}, bf16[64,512]{1,0:T(8,128)(2,1)}, u32[]{:S(2)}) copy-start(bf16[64,512]{1,0:T(8,128)(2,1)} %param.6) | copy-start | bytes 196612
  195.1 15.4 %all-to-all-start.9 = ((bf16[16,2,2048]{2,1,0:T(2,128)(2,1)}), bf16[16,2,2048]{2,1,0:T(2,128)(2,1)S(1)}, u32[]{:S(2)}, u32[]{:S(2)}) async-start(bf16[16,2,2048]{2,1,0:T(2,128)(2,1)} %reshape.53), calls=%async_computation.9 | async-start | bytes 262144 | tf_op jit(solution)/shard_map/all_to_all | solution.py:21
where the time goes:
time: 213 us; the launch traced here: 212 us
  blocking collectives  124 us (58%)
  waiting for transfers between devices  36.6 us (17%)
  starting transfers between devices  19.6 us (9%)
  local copies, waits for them, and re-layouts  13.5 us (6%)
  other arithmetic  12.8 us (6%)
  matrix products  4.54 us (2%)
    all_to_all x5, blocking collectives, sent_to_all(): lax.all_to_all(jnp.broadcast_to(shard[None], (devices, *shard.shape)), ax...  94.8 us
    all_to_all x4, waiting for transfers between devices, sent_to_all(): lax.all_to_all(jnp.broadcast_to(shard[None], (devices, *shard.shape)), ax...  36.6 us
    all_to_all x1, blocking collectives, sum_at_owner(): lax.all_to_all(tiles, axis, split_axis=0, concat_axis=0, tiled=True)  28.8 us
    all_to_all x4, starting transfers between devices, sent_to_all(): lax.all_to_all(jnp.broadcast_to(shard[None], (devices, *shard.shape)), ax...  19.6 us
    unnamed x30, local copies, waits for them, and re-layouts  11.3 us
    all_to_all x6, other arithmetic, sent_to_all(): lax.all_to_all(jnp.broadcast_to(shard[None], (devices, *shard.shape)), ax...  9.57 us
  transfers between devices with their start and end apart: 4, of which 4 were waited for; matrix products, arithmetic and copies ran while one was open for 2% of the time, Pallas kernels for 0%

commit v1 on v0

v1 whole, which is shorter than its diff:
```python
import functools

import jax
import jax.numpy as jnp
from jax import lax
from jax.experimental import pallas as pl
from jax.experimental.pallas import tpu as pltpu
from jax.sharding import PartitionSpec as P

MESH = pl.DeviceIdType.MESH
F32 = jnp.float32
BF16 = jnp.bfloat16


def nt(a, b):
    return lax.dot_general(a, b, (((1,), (1,)), ((), ())), preferred_element_type=F32)


def nn(a, b):
    return jnp.dot(a, b, preferred_element_type=F32)


def kernel(
    ROWS, ZS,
    f_hbm, s_hbm, inv_hbm, link_hbm, rhs_hbm,
    back_ref, rem_ref,
    f_ref, s_ref, inv_ref, link_ref, rhs_ref,
    p_ref, r1_ref, v_ref, r2_ref, piece_ref, strip_ref,
    y_ref, e1_ref, y1_ref, e2_ref, t_ref, e3_ref,
    wl_ref, wr_ref, wm_ref, w_ref, wt_ref,
    lsem, prep_send, prep_recv, rs_send, rs_recv, rr_send, rr_recv,
    g_send, g_recv, l_send, l_recv, e1_send, e1_recv, e2_send, e2_recv, e3_send, e3_recv,
    wr_send, wr_recv, wc_send, wc_recv,
):
    COLS = 2 * ZS
    r = lax.axis_index("row")
    c = lax.axis_index("col")
    z = lax.div(c, 2)
    k = lax.rem(c, 2)
    nrhs, width = s_ref.shape
    bs = f_ref.shape[1]
    block = bs // ZS
    half = block // 2
    per = nrhs // ROWS

    def send(src, dst, ssem, rsem, row, col):
        pltpu.make_async_remote_copy(
            src_ref=src, dst_ref=dst, send_sem=ssem, recv_sem=rsem,
            device_id=(row, col), device_id_type=MESH,
        ).start()

    def local(src, dst, sem):
        pltpu.make_async_copy(src, dst, sem).start()

    def drain(ref, sem):
        pltpu.make_async_copy(ref, ref, sem).wait()

    def other_rows(body):
        def step(i, carry):
            body(lax.rem(r + i, ROWS))
            return carry
        lax.fori_loop(1, ROWS, step, 0)

    def other_zs(body):
        def step(i, carry):
            body(lax.rem(z + i, ZS))
            return carry
        lax.fori_loop(1, ZS, step, 0)

    local(f_hbm.at[0], f_ref.at[0], lsem.at[0])
    local(s_hbm, s_ref, lsem.at[2])
    local(f_hbm.at[1], f_ref.at[1], lsem.at[1])
    local(inv_hbm, inv_ref.at[k], lsem.at[3])
    local(link_hbm, link_ref.at[k], lsem.at[4])
    local(rhs_hbm, rhs_ref.at[k], lsem.at[5])

    barrier = pltpu.get_barrier_semaphore()

    def greet_row(row):
        pl.semaphore_signal(barrier, inc=1, device_id=(row, c), device_id_type=MESH)

    other_rows(greet_row)

    def greet_col(i, carry):
        pl.semaphore_signal(barrier, inc=1, device_id=(r, lax.rem(c + i, COLS)), device_id_type=MESH)
        return carry

    lax.fori_loop(1, COLS, greet_col, 0)

    drain(s_ref, lsem.at[2])
    solved = s_ref[...]
    for which in range(2):
        drain(f_ref.at[which], lsem.at[which])
        part = nt(solved, f_ref[which]).astype(BF16)
        for zz in range(ZS):
            p_ref[which, zz] = part[:, zz * block:(zz + 1) * block]

    pl.semaphore_wait(barrier, ROWS + COLS - 2)

    for which in range(2):
        other_zs(lambda zz: send(
            p_ref.at[which, zz], r1_ref.at[c], rs_send, rs_recv, r, 2 * zz + which))

        @pl.when(k == which)
        def _():
            local(p_ref.at[which, z], r1_ref.at[c], rs_recv)

        @pl.when(k != which)
        def _():
            send(p_ref.at[which, z], r1_ref.at[c], rs_send, rs_recv, r, 2 * z + which)

    mate = 2 * z + (1 - k)
    send(inv_hbm, inv_ref.at[k], prep_send.at[0], prep_recv.at[0], r, mate)
    send(link_hbm, link_ref.at[k], prep_send.at[1], prep_recv.at[1], r, mate)
    send(rhs_hbm, rhs_ref.at[k], prep_send.at[2], prep_recv.at[2], r, mate)
    drain(inv_ref.at[0], lsem.at[3])
    drain(link_ref.at[0], lsem.at[4])
    drain(rhs_ref.at[0], lsem.at[5])
    drain(inv_ref.at[0], prep_recv.at[0])
    drain(link_ref.at[0], prep_recv.at[1])
    drain(rhs_ref.at[0], prep_recv.at[2])

    piece_ref[0] = jnp.concatenate([inv_ref[0, k], inv_ref[1, k]], axis=1)
    rb = link_ref.shape[2]
    eye = (lax.broadcasted_iota(jnp.int32, (rb, rb), 0) == lax.broadcasted_iota(jnp.int32, (rb, rb), 1)).astype(F32).astype(BF16)
    link_cat = jnp.concatenate([link_ref[0], link_ref[1]], axis=0)
    piece_ref[1] = nt(eye, link_cat).astype(BF16)
    strip_ref[0, r] = piece_ref[0]
    other_rows(lambda row: send(piece_ref.at[0], strip_ref.at[0, r], g_send, g_recv, row, c))

    @pl.when(k == 1)
    def _():
        strip_ref[1, r] = piece_ref[1]
        other_rows(lambda row: send(piece_ref.at[1], strip_ref.at[1, r], l_send, l_recv, row, c))

    right = jnp.concatenate([rhs_ref[0, k], rhs_ref[1, k]], axis=0).T
    right = jnp.where(r == 0, right, jnp.zeros_like(right))

    drain(r1_ref, rs_recv)
    total = r1_ref[0].astype(F32)
    for i in range(1, COLS):
        total = total + r1_ref[i].astype(F32)
    value = right - total
    for i in range(ROWS):
        v_ref[i] = value[i * per:(i + 1) * per]
    r2_ref[r] = v_ref[r]
    other_rows(lambda row: send(v_ref.at[row], r2_ref.at[r], rr_send, rr_recv, row, c))
    drain(r2_ref.at[pl.ds(0, ROWS - 1)], rr_recv)
    mine = r2_ref[0]
    for i in range(1, ROWS):
        mine = mine + r2_ref[i]

    strip = strip_ref.at[0]
    drain(strip.at[pl.ds(0, ROWS - 1)], g_recv)

    def strip_of(i):
        return strip_ref[i].reshape(bs, block)

    def summed(ref):
        out = ref[0].astype(F32)
        for i in range(1, ZS):
            out = out + ref[i].astype(F32)
        return out

    def spread_rows(short):
        wl_ref[...] = short
        wr_ref[r] = short
        other_rows(lambda row: send(wl_ref, wr_ref.at[r], wr_send, wr_recv, row, c))

    @pl.when(k == 0)
    def _():
        y_ref[...] = nt(mine.astype(BF16), strip_of(0)).astype(BF16)
        e1_ref[z] = y_ref[...]
        send(y_ref, e1_ref.at[z], e1_send.at[0], e1_recv, r, 2 * z + 1)

        def both(zz):
            send(y_ref, e1_ref.at[z], e1_send.at[0], e1_recv, r, 2 * zz + 1)
            send(y_ref, e1_ref.at[z], e1_send.at[1], e1_recv, r, 2 * zz)

        other_zs(both)
        drain(e1_ref.at[pl.ds(0, ZS - 1)], e1_recv)
        first = summed(e1_ref).astype(BF16).astype(F32)
        drain(e3_ref, e3_recv)
        carry = (first - summed(e3_ref)).astype(BF16)
        spread_rows(nn(carry, strip_of(0)).astype(BF16))
        drain(e1_ref, e1_send.at[0])
        drain(e1_ref.at[pl.ds(0, ZS - 1)], e1_send.at[1])

    @pl.when(k == 1)
    def _():
        drain(strip_ref.at[1, pl.ds(0, ROWS - 1)], l_recv)
        drain(e1_ref, e1_recv)
        first = summed(e1_ref).astype(BF16)
        last_residue = (mine - nn(first, strip_of(1))).astype(BF16)
        y1_ref[...] = nt(last_residue, strip_of(0)).astype(BF16)
        e2_ref[z] = y1_ref[...]
        other_zs(lambda zz: send(y1_ref, e2_ref.at[z], e2_send, e2_recv, r, 2 * zz + 1))
        drain(e2_ref.at[pl.ds(0, ZS - 1)], e2_recv)
        last = summed(e2_ref).astype(BF16)
        short = nn(last, strip_of(0)).astype(BF16)
        t_ref[...] = nt(short, strip_of(1)).astype(BF16)
        send(t_ref, e3_ref.at[z], e3_send, e3_recv, r, 2 * z)
        other_zs(lambda zz: send(t_ref, e3_ref.at[z], e3_send, e3_recv, r, 2 * zz))
        spread_rows(short)
        drain(e2_ref.at[pl.ds(0, ZS - 1)], e2_send)
        drain(e3_ref, e3_send)
        drain(strip_ref.at[1, pl.ds(0, ROWS - 1)], l_send)

    drain(wr_ref.at[pl.ds(0, ROWS - 1)], wr_recv)
    wm_ref[...] = wr_ref[...].reshape(nrhs, block)
    w_ref[k, z] = wm_ref[...]

    def to_cols(which):
        def step(i, carry):
            send(wm_ref, w_ref.at[which, z], wc_send, wc_recv.at[which], r, lax.rem(c + i, COLS))
            return carry
        lax.fori_loop(1, COLS, step, 0)

    def all_of(which):
        return jnp.concatenate([w_ref[which, i] for i in range(ZS)], axis=1)

    def give_back(which):
        wt_ref[...] = w_ref[which, z].astype(F32).T
        back_ref[which] = wt_ref[pl.ds(pl.multiple_of(k * half, half), half), :]

    @pl.when(k == 1)
    def _():
        to_cols(1)
        drain(w_ref.at[1, pl.ds(0, ZS - 1)], wc_recv.at[1])

    @pl.when(k == 0)
    def _():
        to_cols(0)
        drain(w_ref.at[1], wc_recv.at[1])

    rem_ref[...] = s_ref[...].astype(F32) - nn(all_of(1), f_ref[1])
    give_back(1)

    @pl.when(k == 0)
    def _():
        drain(w_ref.at[0, pl.ds(0, ZS - 1)], wc_recv.at[0])

    @pl.when(k == 1)
    def _():
        drain(w_ref.at[0], wc_recv.at[0])

    rem_ref[...] = rem_ref[...] - nn(all_of(0), f_ref[0])
    give_back(0)

    drain(r1_ref.at[pl.ds(0, COLS - 1)], rs_send)
    drain(inv_ref.at[0], prep_send.at[0])
    drain(link_ref.at[0], prep_send.at[1])
    drain(rhs_ref.at[0], prep_send.at[2])
    drain(strip.at[pl.ds(0, ROWS - 1)], g_send)
    drain(r2_ref.at[pl.ds(0, ROWS - 1)], rr_send)
    drain(wr_ref.at[pl.ds(0, ROWS - 1)], wr_send)
    drain(r1_ref.at[pl.ds(0, COLS - 1)], wc_send)


def shards(factor_rows, solved, inverses, link_tile, right_side):
    rows, cols = lax.axis_size("row"), lax.axis_size("col")
    zs = cols // 2
    _, bs, width = factor_rows.shape
    nrhs = solved.shape[0]
    block = bs // zs
    per = nrhs // rows
    _, ih, iw = inverses.shape
    lh, lw = link_tile.shape
    rh = right_side.shape[1]
    dma = pltpu.SemaphoreType.DMA
    any_space = pl.BlockSpec(memory_space=pl.ANY)
    vmem = pl.BlockSpec(memory_space=pltpu.VMEM)
    return pl.pallas_call(
        functools.partial(kernel, rows, zs),
        out_shape=(
            jax.ShapeDtypeStruct((2, rh, nrhs), F32),
            jax.ShapeDtypeStruct((nrhs, width), F32),
        ),
        in_specs=[any_space] * 5,
        out_specs=(vmem, vmem),
        scratch_shapes=[
            pltpu.VMEM((2, bs, width), BF16),
            pltpu.VMEM((nrhs, width), BF16),
            pltpu.VMEM((2, 2, ih, iw), BF16),
            pltpu.VMEM((2, lh, lw), BF16),
            pltpu.VMEM((2, 2, rh, nrhs), F32),
            pltpu.VMEM((2, zs, nrhs, block), BF16),
            pltpu.VMEM((cols, nrhs, block), BF16),
            pltpu.VMEM((rows, per, block), F32),
            pltpu.VMEM((rows, per, block), F32),
            pltpu.VMEM((2, ih, block), BF16),
            pltpu.VMEM((2, rows, ih, block), BF16),
            pltpu.VMEM((per, bs), BF16),
            pltpu.VMEM((zs, per, bs), BF16),
            pltpu.VMEM((per, bs), BF16),
            pltpu.VMEM((zs, per, bs), BF16),
            pltpu.VMEM((per, bs), BF16),
            pltpu.VMEM((zs, per, bs), BF16),
            pltpu.VMEM((per, block), BF16),
            pltpu.VMEM((rows, per, block), BF16),
            pltpu.VMEM((nrhs, block), BF16),
            pltpu.VMEM((2, zs, nrhs, block), BF16),
            pltpu.VMEM((block, nrhs), F32),
            dma((6,)), dma((3,)), dma((3,)), dma, dma, dma, dma,
            dma, dma, dma, dma, dma((2,)), dma, dma, dma, dma, dma,
            dma, dma, dma, dma((2,)),
        ],
        compiler_params=pltpu.CompilerParams(
            collective_id=0, has_side_effects=True, vmem_limit_bytes=32 * 1024 * 1024
        ),
    )(factor_rows, solved, inverses, link_tile, right_side)


def solution(mesh):
    placed = (
        P(None, None, ("row", "col")),
        P(None, ("row", "col")),
        P(None, "row", "col"),
        P("col", "row"),
        P(None, "col", None),
    )
    return jax.shard_map(
        shards,
        mesh=mesh,
        in_specs=placed,
        out_specs=(P(None, "col", None), P(None, ("row", "col"))),
        check_vma=False,
    )
```

time: 213 us -> 65 us (0.31)
  blocking collectives: 124 us -> 0 us
  Pallas kernels: 0 us -> 57.9 us
  waiting for transfers between devices: 36.6 us -> 0 us
  starting transfers between devices: 19.6 us -> 0 us
  other arithmetic: 12.8 us -> 0 us
  local copies, waits for them, and re-layouts: 13.5 us -> 6.06 us
  matrix products: 4.54 us -> 0 us
    all_to_all x6 -> x0, blocking collectives: 124 us -> none  [the longest x5 94.8 us: sent_to_all(): lax.all_to_all(jnp.broadcast_to(shard[None], (devices, *shard.shape)), ax...]
    pallas_call x0 -> x1, Pallas kernels: none -> 57.9 us  [shards(): pl.pallas_call(functools.partial(kernel, rows, zs), out_shape=(jax.ShapeD...]
    all_to_all x4 -> x0, waiting for transfers between devices: 36.6 us -> none  [sent_to_all(): lax.all_to_all(jnp.broadcast_to(shard[None], (devices, *shard.shape)), ax...]
    all_to_all x4 -> x0, starting transfers between devices: 19.6 us -> none  [sent_to_all(): lax.all_to_all(jnp.broadcast_to(shard[None], (devices, *shard.shape)), ax...]
    all_to_all x7 -> x0, other arithmetic: 11.5 us -> none  [the longest x6 9.57 us: sent_to_all(): lax.all_to_all(jnp.broadcast_to(shard[None], (devices, *shard.shape)), ax...]
    unnamed x30 -> x11, local copies, waits for them, and re-layouts: 11.3 us -> 6.06 us
    dot_general x9 -> x0, matrix products: 4.54 us -> none  [the longest x1 2.34 us: shards(): jnp.einsum('kic,nc->kin', factor_rows, solved, preferred_element_type=jnp...]
  transfers between devices with their start and end apart: 4 -> 0, of which waited for: 4 -> 0; matrix products, arithmetic and copies ran while one was open for 2% -> 0% of each run, Pallas kernels for 0% -> 0%
where the time goes in v1:
time: 65 us; the launch traced here: 64.6 us
  Pallas kernels  57.9 us (89%)
  local copies, waits for them, and re-layouts  6.06 us (9%)
  between operations  0.65 us (1%)
    pallas_call x1, Pallas kernels, shards(): pl.pallas_call(functools.partial(kernel, rows, zs), out_shape=(jax.ShapeD...  57.9 us
    unnamed x11, local copies, waits for them, and re-layouts  6.06 us

profile of v1, /device:TPU:1, one launch (start us, length us, event | category | flops | bytes accessed | tf_op | source)
XLA Modules:
  0.0 64.6 jit_solution(508136570174734644)
XLA Ops:
  0.6 0.8 %copy.7.link_hbm = bf16[64,32]{1,0:T(8,128)(2,1)S(1)} copy(bf16[64,32]{0,1:T(8,128)(2,1)} %param.8) | data formatting | bytes 8192 | tf_op args[3]
  1.4 0.0 copy-start
  1.4 1.6 %copy-done = bf16[2,1024,512]{2,1,0:T(8,128)(2,1)S(1)} copy-done((bf16[2,1024,512]{2,1,0:T(8,128)(2,1)S(1)}, bf16[2,1024,512]{2,1,0:T(8,128)(2,1)}, u32[]{:S(2)}) %copy-start) | copy-done | bytes 2097176
  3.0 0.0 copy-start.1
  3.0 0.8 %copy-done.1 = bf16[64,512]{1,0:T(8,128)(2,1)S(1)} copy-done((bf16[64,512]{1,0:T(8,128)(2,1)S(1)}, bf16[64,512]{1,0:T(8,128)(2,1)}, u32[]{:S(2)}) %copy-start.1) | copy-done | bytes 65560
  3.9 0.0 copy-start.2
  3.9 0.8 %copy-done.2 = f32[2,64,64]{2,1,0:T(8,128)S(1)} copy-done((f32[2,64,64]{2,1,0:T(8,128)S(1)}, f32[2,64,64]{2,1,0:T(8,128)}, u32[]{:S(2)}) %copy-start.2) | copy-done | bytes 32792
  4.7 0.0 copy-start.3
  4.7 0.7 %copy-done.3 = bf16[2,32,64]{2,1,0:T(8,128)(2,1)S(1)} copy-done((bf16[2,32,64]{2,1,0:T(8,128)(2,1)S(1)}, bf16[2,32,64]{2,1,0:T(8,128)(2,1)}, u32[]{:S(2)}) %copy-start.3) | copy-done | bytes 8216
  5.4 57.9 %shard_map.68 = (f32[2,64,64]{2,1,0:T(8,128)S(1)}, f32[64,512]{1,0:T(8,128)S(1)}) custom-call(bf16[2,1024,512]{2,1,0:T(8,128)(2,1)S(1)} %copy-done, bf16[64,512]{1,0:T(8,128)(2,1)S(1)} %copy-done.1, bf16[2,32,64]{2,1,0:T(8,128)(2,1)S(1)} %copy-done.3, bf16[64,32]{1,0:T(8,128)(2,1)S(1)} %copy.7.link_hbm, f32[2,64,64]{2,1,0:T(8,128)S(1)} %copy-done.2), custom_call_target="tpu_custom_call" | custom-call | tf_op jit(solution)/shard_map/pallas_call | solution.py:273
  63.3 0.6 copy.10
  64.0 0.7 %copy.11 = f32[64,512]{1,0:T(8,128)} copy(f32[64,512]{1,0:T(8,128)S(1)} %get-tuple-element.5) | data formatting | bytes 262144
Async XLA Ops:
  1.4 1.6 %copy-start = (bf16[2,1024,512]{2,1,0:T(8,128)(2,1)S(1)}, bf16[2,1024,512]{2,1,0:T(8,128)(2,1)}, u32[]{:S(2)}) copy-start(bf16[2,1024,512]{2,1,0:T(8,128)(2,1)} %f_hbm.1) | copy-start | bytes 6291460
  3.0 0.8 %copy-start.1 = (bf16[64,512]{1,0:T(8,128)(2,1)S(1)}, bf16[64,512]{1,0:T(8,128)(2,1)}, u32[]{:S(2)}) copy-start(bf16[64,512]{1,0:T(8,128)(2,1)} %s_hbm.1) | copy-start | bytes 196612
  3.9 0.8 %copy-start.2 = (f32[2,64,64]{2,1,0:T(8,128)S(1)}, f32[2,64,64]{2,1,0:T(8,128)}, u32[]{:S(2)}) copy-start(f32[2,64,64]{2,1,0:T(8,128)} %rhs_hbm.1) | copy-start | bytes 98308
  4.7 0.7 %copy-start.3 = (bf16[2,32,64]{2,1,0:T(8,128)(2,1)S(1)}, bf16[2,32,64]{2,1,0:T(8,128)(2,1)}, u32[]{:S(2)}) copy-start(bf16[2,32,64]{2,1,0:T(8,128)(2,1)} %inv_hbm.1) | copy-start | bytes 24580

commit v2 on v1

--- a/solution.py
+++ b/solution.py
@@ -121,10 +121,7 @@
     drain(rhs_ref.at[0], prep_recv.at[2])
 
     piece_ref[0] = jnp.concatenate([inv_ref[0, k], inv_ref[1, k]], axis=1)
-    rb = link_ref.shape[2]
-    eye = (lax.broadcasted_iota(jnp.int32, (rb, rb), 0) == lax.broadcasted_iota(jnp.int32, (rb, rb), 1)).astype(F32).astype(BF16)
-    link_cat = jnp.concatenate([link_ref[0], link_ref[1]], axis=0)
-    piece_ref[1] = nt(eye, link_cat).astype(BF16)
+    piece_ref[1] = jnp.concatenate([link_ref[0], link_ref[1]], axis=1)
     strip_ref[0, r] = piece_ref[0]
     other_rows(lambda row: send(piece_ref.at[0], strip_ref.at[0, r], g_send, g_recv, row, c))
 
@@ -282,7 +279,7 @@
             pltpu.VMEM((2, bs, width), BF16),
             pltpu.VMEM((nrhs, width), BF16),
             pltpu.VMEM((2, 2, ih, iw), BF16),
-            pltpu.VMEM((2, lh, lw), BF16),
+            pltpu.VMEM((2, lw, lh), BF16),
             pltpu.VMEM((2, 2, rh, nrhs), F32),
             pltpu.VMEM((2, zs, nrhs, block), BF16),
             pltpu.VMEM((cols, nrhs, block), BF16),
@@ -306,9 +303,9 @@
             dma, dma, dma, dma((2,)),
         ],
         compiler_params=pltpu.CompilerParams(
-            collective_id=0, has_side_effects=True, vmem_limit_bytes=32 * 1024 * 1024
+            collective_id=0, has_side_effects=True, vmem_limit_bytes=60 * 1024 * 1024
         ),
-    )(factor_rows, solved, inverses, link_tile, right_side)
+    )(factor_rows, solved, inverses, link_tile.T, right_side)
 
 
 def solution(mesh):

time: 65 us -> 62.1 us (0.955)
  local copies, waits for them, and re-layouts: 6.06 us -> 3.04 us
    unnamed x11 -> x2, local copies, waits for them, and re-layouts: 6.06 us -> 3.04 us
where the time goes in v2:
time: 62.1 us; the launch traced here: 61.9 us
  Pallas kernels  58.3 us (94%)
  local copies, waits for them, and re-layouts  3.04 us (5%)
  between operations  0.64 us (1%)
    pallas_call x1, Pallas kernels, shards(): pl.pallas_call(functools.partial(kernel, rows, zs), out_shape=(jax.ShapeD...  58.3 us
    unnamed x2, local copies, waits for them, and re-layouts  3.04 us

profile of v2, /device:TPU:1, one launch (start us, length us, event | category | flops | bytes accessed | tf_op | source)
XLA Modules:
  0.0 61.9 jit_solution(14383379582067042219)
XLA Ops:
  0.6 58.3 %shard_map.68 = (f32[2,64,64]{2,1,0:T(8,128)}, f32[64,512]{1,0:T(8,128)}) custom-call(bf16[2,1024,512]{2,1,0:T(8,128)(2,1)} %f_hbm.1, bf16[64,512]{1,0:T(8,128)(2,1)} %s_hbm.1, bf16[2,32,64]{2,1,0:T(8,128)(2,1)} %inv_hbm.1, bf16[32,64]{1,0:T(8,128)(2,1)} %bitcast.1, f32[2,64,64]{2,1,0:T(8,128)} %rhs_hbm.1), custom_call_target="tpu_custom_call" | custom-call | tf_op jit(solution)/shard_map/pallas_call | solution.py:270
  58.9 1.5 %copy.9 = f32[2,64,64]{2,1,0:T(8,128)} copy(f32[2,64,64]{2,1,0:T(8,128)} %get-tuple-element.4) | data formatting | bytes 65536
  60.4 1.6 %copy.10 = f32[64,512]{1,0:T(8,128)} copy(f32[64,512]{1,0:T(8,128)} %get-tuple-element.5) | data formatting | bytes 262144
